TPU v7x, 512 devices: a whole 4x4x16 slice. The times are simulated.
512 devices in a mesh: section: 4 (over x), dp: 4 (over y), tensor: 32 (over z, core).
Axes of the slice: x: 4, y: 4, z: 16, core: 2. Of those that a mesh axis runs over, the one named last changes fastest.
Arguments:
- activations: bfloat16 [512, 8192], P('dp', 'tensor'), may hold values from -6 to 6
- targets: bfloat16 [4, 512, 8192], P('section', 'dp', 'tensor'), may hold values from -12 to 12
- packed_floors: int32 [4, 2048, 8192], P('section', 'dp', 'tensor'), may hold values from 0 to 4095
- rounding: float32 [4, 8192, 8192], P('section', 'dp', 'tensor'), may hold values from -8 to 8
- scales: float32 [4, 8192], P('section', 'tensor'), may hold values from 0.001 to 0.006
- norm_gains: float32 [4, 8192], P('section'), may hold values from 0.5 to 1.5
Outputs:
- rounding_next: float32 [4, 8192, 8192], P('section', 'dp', 'tensor')
- block_outputs: bfloat16 [4, 512, 8192], P('section', 'dp', 'tensor')
- losses: float32 [4], P('section')
Inputs may be any that keep to these rules, and one draw needn't show every extreme that they name: `packed_floors`: each word holds four 3-bit codes in its lowest 12 bits, lowest bits first: code k of word r of a column is row 4 r + k; the floor is the code minus 4.
All inputs are finite; a program needn't handle non-finite values.
Results may differ from a plain program's by a relative error of at most 0.0045.
The roundings to bfloat16 on the way count: a program that leaves them out, or rounds other values in their place, can miss the bound.
Values may be sent and summed in bfloat16 or wider, within the bound.
No kernel may reach another device: no remote copies, remote signals or barrier semaphores. Data moves between devices by JAX's collectives and lax.ppermute only.
A program may use at most 64 MiB of HBM per device.

v0:
```python
import jax
import jax.numpy as jnp
from jax import lax
from jax.sharding import Mesh
from jax.sharding import PartitionSpec as P

TENSOR = ("tensor_0", "tensor_1")
PLANE = ("section", "dp")
norm_eps = 1e-06
grad_eps = 1e-06
reg_weight = 0.3
step_rate = 0.25
error_scale = 600.0


def exchange(x, axes):
    return lax.all_to_all(x, axes, 0, 0, tiled=True)


def total_over(x, axes):
    peers = 1
    for axis in axes if isinstance(axes, tuple) else (axes,):
        peers *= lax.axis_size(axis)
    return jnp.sum(exchange(jnp.broadcast_to(x[None], (peers, *x.shape)), axes), axis=0)


def unpack(words):
    shifts = 3 * jnp.arange(4, dtype=jnp.int32)
    codes = jnp.right_shift(words[:, None, :], shifts[None, :, None]) & 7
    return codes.reshape(words.shape[0] * 4, words.shape[1]).astype(jnp.float32) - 4.0


def soft_round(values):
    sig = jax.nn.sigmoid(values)
    linear = 1.2 * sig - 0.1
    soft_part = jnp.clip(linear, 0.0, 1.0)
    soft_slope = jnp.where((linear > 0.0) & (linear < 1.0), 1.2 * sig * (1.0 - sig), 0.0)
    return (soft_part, soft_slope)


def per_device(activations, targets, packed_floors, rounding, scales, norm_gains):
    sections = lax.axis_size("section")
    dps = lax.axis_size("dp")
    tensors = lax.axis_size("tensor_0") * lax.axis_size("tensor_1")
    section_index = lax.axis_index("section")
    dp_index = lax.axis_index("dp")
    tok_dev, width_local = activations.shape
    width_full = norm_gains.shape[1]
    token_total = tok_dev * dps
    rows_local = width_full // dps
    near = tensors // dps
    own = width_local // dps
    tok_part = tok_dev // sections
    tok_group = tok_part * dps
    soft_part, soft_slope = soft_round(rounding[0])
    channel_scale = scales[0][None, :]
    weight = (channel_scale * (unpack(packed_floors[0]) + soft_part)).astype(jnp.bfloat16)
    weight = weight.reshape(near, dps, own, width_local).transpose(1, 0, 2, 3)
    weight = exchange(weight.reshape(dps, near * own, width_local), "dp")
    weights = lax.all_gather(weight.reshape(rows_local, width_local), "section", axis=0)
    gains_own = norm_gains[0].reshape(tensors, dps, own)
    gains_own = lax.dynamic_index_in_dim(gains_own, dp_index, 1, keepdims=False).reshape(
        1, rows_local
    )
    gains = lax.all_gather(gains_own, "section", axis=0, tiled=True)
    fresh = lax.dynamic_slice_in_dim(activations, section_index * tok_part, tok_part, 0)
    fresh = exchange(fresh.reshape(tok_part, dps, own).transpose(1, 0, 2), "dp")
    current = fresh.reshape(tok_group, own).T
    target_all = lax.all_gather(targets[0], "dp", axis=0)
    target_all = target_all.reshape(dps, sections, tok_part, width_local).transpose(1, 0, 2, 3)
    target_all = target_all.reshape(token_total, width_local).astype(jnp.float32)
    sent = []
    for block in range(sections):
        features = lax.all_gather(current, TENSOR, axis=0, tiled=True).astype(jnp.float32)
        gain = gains[block][:, None]
        scaled = (features * gain).astype(jnp.bfloat16)
        partial = lax.dot_general(
            weights[block], scaled, (((0,), (0,)), ((), ())), preferred_element_type=jnp.float32
        )
        squares = jnp.sum(features * features, axis=0)
        piece = jnp.concatenate(
            [
                partial.reshape(dps, own, tok_group),
                jnp.broadcast_to(squares[None, None], (dps, 8, tok_group)),
            ],
            axis=1,
        )
        summed = jnp.sum(exchange(piece, "dp"), axis=0)
        rate = lax.rsqrt(summed[own : own + 1] / width_full + norm_eps)
        current = (current.astype(jnp.float32) + rate * summed[:own]).astype(jnp.bfloat16)
        normed = (features * rate * gain).astype(jnp.bfloat16)
        sent.append(
            jnp.concatenate(
                [
                    normed.reshape(dps, near * own, tok_group),
                    jnp.broadcast_to(current[None], (dps, own, tok_group)),
                ],
                axis=1,
            )
        )
    came = exchange(jnp.concatenate(sent, axis=0), PLANE)
    came = came.reshape(sections, dps, near * own + own, tok_group)
    rows = came[:, :, : near * own].reshape(sections, dps, near, own, tok_group)
    rows = rows.transpose(2, 1, 3, 0, 4).reshape(rows_local, token_total)
    result = came[:, :, near * own :].transpose(0, 3, 1, 2).reshape(token_total, width_local)
    residue = result.astype(jnp.float32) - target_all
    delta = (error_scale / token_total**0.5 * residue).astype(jnp.bfloat16)
    grad_w = jnp.dot(rows, delta, preferred_element_type=jnp.float32)
    polarity = 2.0 * soft_part - 1.0
    grad = soft_slope * (channel_scale * grad_w - 8.0 * reg_weight * polarity**3)
    sums = jnp.stack(
        [jnp.sum(residue * residue) / dps, jnp.sum(1.0 - polarity**4), jnp.sum(grad * grad)]
    )
    sums = jnp.broadcast_to(jnp.pad(sums, (0, 5))[:, None], (8, 128))
    sums = total_over(total_over(sums, TENSOR), "dp")[:, 0]
    mean_grad = sums[2] / (width_full * width_full) + grad_eps
    rounding_next = rounding[0] - step_rate * grad * lax.rsqrt(mean_grad)
    loss_value = sums[0] / (token_total * width_full) + reg_weight * sums[1] / (
        width_full * width_full
    )
    outputs = lax.dynamic_index_in_dim(
        result.reshape(sections, dps, tok_part, width_local), dp_index, 1, keepdims=False
    )
    return (rounding_next[None], outputs.reshape(1, tok_dev, width_local), loss_value.reshape(1))


def solution(mesh):
    torus = Mesh(
        mesh.devices.reshape(mesh.shape["section"], mesh.shape["dp"], 16, 2),
        ("section", "dp", "tensor_0", "tensor_1"),
    )
    return jax.shard_map(
        per_device,
        mesh=torus,
        in_specs=(
            P("dp", TENSOR),
            P("section", "dp", TENSOR),
            P("section", "dp", TENSOR),
            P("section", "dp", TENSOR),
            P("section", TENSOR),
            P("section", None),
        ),
        out_specs=(P("section", "dp", TENSOR), P("section", "dp", TENSOR), P("section")),
        check_vma=False,
    )
```

profile of v0, /device:TPU:4, one launch (start us, length us, event | category | flops | bytes accessed | tf_op | source)
XLA Modules:
  0.0 358.8 jit_solution(6779789227103633169)
XLA Ops:
  7.2 2.7 shift_right_arithmetic.24
  10.0 3.1 shift_right_arithmetic.25
  13.1 1.9 add_clamp_fusion
  15.1 2.8 fusion.27
  18.0 19.5 %all_to_all.45 = bf16[4,512,256]{2,1,0:T(8,128)(2,1)} all-to-all(bf16[4,512,256]{2,1,0:T(8,128)(2,1)S(1)} %bitcast.124), channel_id=1, replica_groups=mesh['section'=4,'dp'=4,'tensor_0'=16,'tensor_1'=2] {'dp'}, dimensions={0} | all-to-all | bytes 2097152 | tf_op jit(solution)/shard_map/all_to_all | solution.py:17
  37.6 0.7 reshape.171
  38.3 3.3 all-to-all-start
  41.6 0.5 broadcast.139
  42.1 0.7 reduce.4
  43.0 10.7 %all-gather = f32[4,1,2048]{2,1,0:T(1,128)S(1)} all-gather(f32[1,1,2048]{2,1,0:T(1,128)S(1)} %reshape.147), channel_id=1, replica_groups=mesh['section'=4,'dp'=4,'tensor_0'=16,'tensor_1'=2] {'section'}, dimensions={0}, use_global_device_ids=true | all-gather | bytes 40960 | tf_op jit(solution)/shard_map/all_gather | solution.py:65
  53.9 37.7 %all_gather.21 = bf16[2048,128]{1,0:T(8,128)(2,1)S(1)} all-gather(bf16[64,128]{1,0:T(8,128)(2,1)S(1)} %bitcast.137), channel_id=1, replica_groups=mesh['section'=4,'dp'=4,'tensor_0'=16,'tensor_1'=2] {'tensor_0','tensor_1'}, dimensions={0}, use_global_device_ids=true | all-gather | bytes 540672 | tf_op jit(solution)/shard_map/all_gather | solution.py:74
  91.6 0.3 fusion.12
  91.8 3.2 all-gather.3.cloned.1.call-done
  95.0 4.3 %slice_bitcast_fusion = (bf16[256,2048]{0,1:T(8,128)(2,1)}, bf16[256,2048]{0,1:T(8,128)(2,1)}, bf16[256,2048]{0,1:T(8,128)(2,1)}, bf16[256,2048]{0,1:T(8,128)(2,1)}) fusion(bf16[4,2048,256]{2,1,0:T(8,128)(2,1)} %all-gather.3.cloned.1.call-done), kind=kLoop, calls=%fused_computation.50 | loop fusion | bytes 8388608 | tf_op jit(solution)/shard_map/dot_general | solution.py:77
  99.3 2.3 copy.54
  101.6 1.8 fusion.38
  103.4 0.7 pad_maximum_fusion
  104.0 4.3 %all-to-all-start.2 = ((f32[4,72,128]{2,1,0:T(8,128)}), f32[4,72,128]{2,1,0:T(8,128)S(1)}, u32[]{:S(2)}, u32[]{:S(2)}) async-start(f32[4,72,128]{2,1,0:T(8,128)} %pad_maximum_fusion), calls=%async_computation.2 | async-start | bytes 294912 | tf_op jit(solution)/shard_map/all_to_all | solution.py:17
  108.3 2.3 copy.56
  110.6 2.3 copy.57
  112.9 2.3 copy.58
  115.2 32.4 %all_gather.24 = bf16[2048,128]{1,0:T(8,128)(2,1)S(1)} all-gather(bf16[64,128]{1,0:T(8,128)(2,1)S(1)} %fusion.53), channel_id=1, replica_groups=mesh['section'=4,'dp'=4,'tensor_0'=16,'tensor_1'=2] {'tensor_0','tensor_1'}, dimensions={0}, use_global_device_ids=true | all-gather | bytes 540672 | tf_op jit(solution)/shard_map/all_gather | solution.py:74
  147.9 1.8 fusion.35
  149.7 0.7 pad_maximum_fusion.1
  150.4 4.8 %all-to-all-start.3 = ((f32[4,72,128]{2,1,0:T(8,128)}), f32[4,72,128]{2,1,0:T(8,128)S(1)}, u32[]{:S(2)}, u32[]{:S(2)}) async-start(f32[4,72,128]{2,1,0:T(8,128)} %pad_maximum_fusion.1), calls=%async_computation.3 | async-start | bytes 294912 | tf_op jit(solution)/shard_map/all_to_all | solution.py:17
  155.2 1.1 fusion.14
  156.3 4.9 %all-to-all-done.3 = f32[4,72,128]{2,1,0:T(8,128)S(1)} async-done(((f32[4,72,128]{2,1,0:T(8,128)}), f32[4,72,128]{2,1,0:T(8,128)S(1)}, u32[]{:S(2)}, u32[]{:S(2)}) %all-to-all-start.3) | async-done | bytes 147488 | tf_op jit(solution)/shard_map/all_to_all | solution.py:17
  161.3 29.5 %all_gather.25 = bf16[2048,128]{1,0:T(8,128)(2,1)S(1)} all-gather(bf16[64,128]{1,0:T(8,128)(2,1)S(1)} %fusion.51), channel_id=1, replica_groups=mesh['section'=4,'dp'=4,'tensor_0'=16,'tensor_1'=2] {'tensor_0','tensor_1'}, dimensions={0}, use_global_device_ids=true | all-gather | bytes 540672 | tf_op jit(solution)/shard_map/all_gather | solution.py:74
  191.1 1.8 fusion.32
  192.9 0.7 pad_maximum_fusion.2
  193.6 3.3 all-to-all-start.4
  196.9 1.1 fusion.18
  198.1 5.0 %all-to-all-done.4 = f32[4,72,128]{2,1,0:T(8,128)S(1)} async-done(((f32[4,72,128]{2,1,0:T(8,128)}), f32[4,72,128]{2,1,0:T(8,128)S(1)}, u32[]{:S(2)}, u32[]{:S(2)}) %all-to-all-start.4) | async-done | bytes 147488 | tf_op jit(solution)/shard_map/all_to_all | solution.py:17
  203.2 30.0 %all_gather.26 = bf16[2048,128]{1,0:T(8,128)(2,1)S(1)} all-gather(bf16[64,128]{1,0:T(8,128)(2,1)S(1)} %fusion.49), channel_id=1, replica_groups=mesh['section'=4,'dp'=4,'tensor_0'=16,'tensor_1'=2] {'tensor_0','tensor_1'}, dimensions={0}, use_global_device_ids=true | all-gather | bytes 540672 | tf_op jit(solution)/shard_map/all_gather | solution.py:74
  233.5 1.8 fusion.29
  235.3 0.7 pad_maximum_fusion.3
  236.0 3.5 all-to-all-start.5
  239.5 1.1 fusion.22
  240.6 4.9 %all-to-all-done.5 = f32[4,72,128]{2,1,0:T(8,128)S(1)} async-done(((f32[4,72,128]{2,1,0:T(8,128)}), f32[4,72,128]{2,1,0:T(8,128)S(1)}, u32[]{:S(2)}, u32[]{:S(2)}) %all-to-all-start.5) | async-done | bytes 147488 | tf_op jit(solution)/shard_map/all_to_all | solution.py:17
  245.5 0.3 fusion.26
  245.9 6.8 %maximum_maximum_fusion = bf16[16,576,128]{2,1,0:T(8,128)(2,1)} fusion(bf16[4,64,128]{2,1,0:T(8,128)(2,1)S(1)} %broadcast_in_dim.29, bf16[4,512,128]{2,1,0:T(8,128)(2,1)S(1)} %bitcast.128, bf16[4,64,128]{2,1,0:T(8,128)(2,1)S(1)} %broadcast_in_dim.27, bf16[4,512,128]{2,1,0:T(8,128)(2,1)} %bitcast.127, bf16[4,64,128]{2,1,0:T(8,128)(2,1)S(1)} %broadcast_in_dim.25, ...), kind=kLoop, calls=%fused_computation.5 | loop fusion | flops 18874368 | bytes 4718592 | tf_op jit(solution)/shard_map/concatenate | solution.py:101
  252.8 5.8 %all-to-all-start.6 = ((bf16[16,576,128]{2,1,0:T(8,128)(2,1)}), bf16[16,576,128]{2,1,0:T(8,128)(2,1)}, u32[]{:S(2)}, u32[]{:S(2)}) async-start(bf16[16,576,128]{2,1,0:T(8,128)(2,1)} %maximum_maximum_fusion), calls=%async_computation.6 | async-start | bytes 4718592 | tf_op jit(solution)/shard_map/all_to_all | solution.py:17
  258.6 35.7 %all_gather.27 = bf16[4,128,256]{2,1,0:T(8,128)(2,1)S(1)} all-gather(bf16[1,128,256]{2,1,0:T(8,128)(2,1)S(1)} %copy-done.3), channel_id=1, replica_groups=mesh['section'=4,'dp'=4,'tensor_0'=16,'tensor_1'=2] {'dp'}, dimensions={0}, use_global_device_ids=true | all-gather | bytes 327680 | tf_op jit(solution)/shard_map/all_gather | solution.py:69
  294.3 0.8 copy_bitcast_fusion
  295.1 1.5 reshape.140
  296.6 1.1 copy.61
  297.7 1.5 fusion.4
  299.2 1.7 slice.111
  301.0 2.0 copy.59
  303.0 1.7 multiply_reduce_fusion.1
  304.9 3.9 %multiply_reduce_fusion = (f32[]{:T(128)}, f32[2048,256]{1,0:T(8,128)}) fusion(bf16[32,8,4,128]{3,2,1,0:T(4,128)(2,1)S(1)} %bitcast.136, bf16[256,8,4,128]{3,2,1,0:T(4,128)(2,1)S(1)} %bitcast.129, f32[256]{0:T(256)S(1)} %bitcast.151, f32[1,2048,256]{2,1,0:T(8,128)S(1)} %copy-done.1), kind=kOutput, calls=%fused_computation.18 | convolution fusion | flops 548405248 | bytes 6554628 | tf_op jit(solution)/shard_map/dot_general | solution.py:108
  309.4 1.3 select_maximum_fusion
  310.7 0.7 broadcast_in_dim_broadcast_in_dim_broadcast_in_dim.2
  311.4 7.3 %all-to-all-start.7 = ((f32[32,8,128]{2,1,0:T(8,128)}), f32[32,8,128]{2,1,0:T(8,128)S(1)}, u32[]{:S(2)}, u32[]{:S(2)}) async-start(f32[32,8,128]{2,1,0:T(8,128)} %broadcast_in_dim_broadcast_in_dim_broadcast_in_dim.2), calls=%async_computation.7 | async-start | bytes 262144 | tf_op jit(solution)/shard_map/all_to_all | solution.py:17
  318.7 1.0 slice_bitcast_fusion.4
  319.7 0.3 copy.63
  320.0 0.3 reshape_reshape.3
  320.3 15.6 %all-to-all-done.7 = f32[32,8,128]{2,1,0:T(8,128)S(1)} async-done(((f32[32,8,128]{2,1,0:T(8,128)}), f32[32,8,128]{2,1,0:T(8,128)S(1)}, u32[]{:S(2)}, u32[]{:S(2)}) %all-to-all-start.7) | async-done | bytes 131104 | tf_op jit(solution)/shard_map/all_to_all | solution.py:17
  336.0 0.6 broadcast_in_dim.30
  336.6 3.2 all-to-all-start.8
  339.8 0.6 constant_dynamic-slice_fusion
  340.5 4.7 %all-to-all-done.8 = f32[4,8,128]{2,1,0:T(8,128)S(1)} async-done(((f32[4,8,128]{2,1,0:T(8,128)}), f32[4,8,128]{2,1,0:T(8,128)S(1)}, u32[]{:S(2)}, u32[]{:S(2)}) %all-to-all-start.8) | async-done | bytes 16416 | tf_op jit(solution)/shard_map/all_to_all | solution.py:17
  345.1 0.6 fusion.67
  347.7 3.2 fusion.10
  (56 shorter events, 2.0 us)
Async XLA Ops:
  7.2 30.3 %copy-start = (bf16[128,256]{1,0:T(8,128)(2,1)S(1)}, bf16[128,256]{1,0:T(8,128)(2,1)}, u32[]{:S(2)}) copy-start(bf16[128,256]{1,0:T(8,128)(2,1)} %param.6) | copy-start | bytes 196612
  7.2 87.8 %all-gather.3.cloned.1.call-start = ((), (), s32[]{:S(2)}) async-start(), calls=%async_computation.9 | async-start | bytes 5242880 | tf_op jit(solution)/shard_map/all_gather | solution.py:60
  10.0 3.1 copy-start.1
  13.1 2.0 copy-start.5
  18.0 24.1 %copy-start.4 = (f32[1,8192]{1,0:T(1,128)S(1)}, f32[1,8192]{1,0:T(1,128)}, u32[]{:S(2)}) copy-start(f32[1,8192]{1,0:T(1,128)} %param.11) | copy-start | bytes 98308
  38.3 15.4 %all-to-all-start = ((bf16[4,2,1024]{2,1,0:T(2,128)(2,1)}), bf16[4,2,1024]{2,1,0:T(2,128)(2,1)S(1)}, u32[]{:S(2)}, u32[]{:S(2)}) async-start(bf16[4,2,1024]{2,1,0:T(2,128)(2,1)} %reshape.171), calls=%async_computation | async-start | bytes 32768 | tf_op jit(solution)/shard_map/all_to_all | solution.py:17
  104.0 11.1 %all-to-all-start.2 = ((f32[4,72,128]{2,1,0:T(8,128)}), f32[4,72,128]{2,1,0:T(8,128)S(1)}, u32[]{:S(2)}, u32[]{:S(2)}) async-start(f32[4,72,128]{2,1,0:T(8,128)} %pad_maximum_fusion), calls=%async_computation.2 | async-start | bytes 294912 | tf_op jit(solution)/shard_map/all_to_all | solution.py:17
  150.4 10.9 %all-to-all-start.3 = ((f32[4,72,128]{2,1,0:T(8,128)}), f32[4,72,128]{2,1,0:T(8,128)S(1)}, u32[]{:S(2)}, u32[]{:S(2)}) async-start(f32[4,72,128]{2,1,0:T(8,128)} %pad_maximum_fusion.1), calls=%async_computation.3 | async-start | bytes 294912 | tf_op jit(solution)/shard_map/all_to_all | solution.py:17
  193.6 9.5 %all-to-all-start.4 = ((f32[4,72,128]{2,1,0:T(8,128)}), f32[4,72,128]{2,1,0:T(8,128)S(1)}, u32[]{:S(2)}, u32[]{:S(2)}) async-start(f32[4,72,128]{2,1,0:T(8,128)} %pad_maximum_fusion.2), calls=%async_computation.4 | async-start | bytes 294912 | tf_op jit(solution)/shard_map/all_to_all | solution.py:17
  236.0 9.5 %all-to-all-start.5 = ((f32[4,72,128]{2,1,0:T(8,128)}), f32[4,72,128]{2,1,0:T(8,128)S(1)}, u32[]{:S(2)}, u32[]{:S(2)}) async-start(f32[4,72,128]{2,1,0:T(8,128)} %pad_maximum_fusion.3), calls=%async_computation.5 | async-start | bytes 294912 | tf_op jit(solution)/shard_map/all_to_all | solution.py:17
  252.8 5.8 %copy-start.3 = (bf16[1,128,256]{2,1,0:T(8,128)(2,1)S(1)}, bf16[1,128,256]{2,1,0:T(8,128)(2,1)}, u32[]{:S(2)}) copy-start(bf16[1,128,256]{2,1,0:T(8,128)(2,1)} %param.7) | copy-start | bytes 196612
  252.8 46.4 %all-to-all-start.6 = ((bf16[16,576,128]{2,1,0:T(8,128)(2,1)}), bf16[16,576,128]{2,1,0:T(8,128)(2,1)}, u32[]{:S(2)}, u32[]{:S(2)}) async-start(bf16[16,576,128]{2,1,0:T(8,128)(2,1)} %maximum_maximum_fusion), calls=%async_computation.6 | async-start | bytes 4718592 | tf_op jit(solution)/shard_map/all_to_all | solution.py:17
  301.0 2.0 copy-start.2
  311.4 24.5 %all-to-all-start.7 = ((f32[32,8,128]{2,1,0:T(8,128)}), f32[32,8,128]{2,1,0:T(8,128)S(1)}, u32[]{:S(2)}, u32[]{:S(2)}) async-start(f32[32,8,128]{2,1,0:T(8,128)} %broadcast_in_dim_broadcast_in_dim_broadcast_in_dim.2), calls=%async_computation.7 | async-start | bytes 262144 | tf_op jit(solution)/shard_map/all_to_all | solution.py:17
  336.6 8.6 %all-to-all-start.8 = ((f32[4,8,128]{2,1,0:T(8,128)}), f32[4,8,128]{2,1,0:T(8,128)S(1)}, u32[]{:S(2)}, u32[]{:S(2)}) async-start(f32[4,8,128]{2,1,0:T(8,128)} %broadcast_in_dim.30), calls=%async_computation.8 | async-start | bytes 32768 | tf_op jit(solution)/shard_map/all_to_all | solution.py:17
Sparse Core Ops, SparseCore 0:
  37.6 57.3 all-gather.2
where the time goes:
time: 360 us; the launch traced here: 359 us
  blocking collectives  196 us (54%)
  waiting for transfers between devices  38.3 us (11%)
  starting transfers between devices  35.6 us (10%)
  local copies, waits for them, and re-layouts  31.9 us (9%)
  other arithmetic  28.4 us (8%)
  between operations  18.2 us (5%)
  matrix products  11 us (3%)
    all_gather x4, blocking collectives, per_device(): lax.all_gather(current, TENSOR, axis=0, tiled=True).astype(jnp.float32)  130 us
    all_gather x1, blocking collectives, per_device(): target_all = lax.all_gather(targets[0], 'dp', axis=0)  35.7 us
    all_to_all x8, starting transfers between devices, exchange(): return lax.all_to_all(x, axes, 0, 0, tiled=True)  35.5 us
    all_to_all x8, waiting for transfers between devices, exchange(): return lax.all_to_all(x, axes, 0, 0, tiled=True)  35.1 us
    all_to_all x1, blocking collectives, exchange(): return lax.all_to_all(x, axes, 0, 0, tiled=True)  19.5 us
    dot_general x5, local copies, waits for them, and re-layouts, per_device(): lax.dot_general(weights[block], scaled, (((0,), (0,)), ((), ())), preferr...  13.4 us
    all_gather x1, blocking collectives, per_device(): gains = lax.all_gather(gains_own, 'section', axis=0, tiled=True)  10.7 us
  transfers between devices with their start and end apart: 9, of which 6 were waited for; matrix products, arithmetic and copies ran while one was open for 6% of the time, Pallas kernels for 0%

commit v1 on v0

--- a/solution.py
+++ b/solution.py
@@ -3,6 +3,7 @@
 from jax import lax
 from jax.sharding import Mesh
 from jax.sharding import PartitionSpec as P
+from jax.lax import all_to_all, axis_size
 
 TENSOR = ("tensor_0", "tensor_1")
 PLANE = ("section", "dp")
@@ -11,6 +12,18 @@
 reg_weight = 0.3
 step_rate = 0.25
 error_scale = 600.0
+
+
+def _prepare_vectors(packet):
+    return jnp.concatenate(
+        all_to_all(
+            jnp.stack(tuple((packet for _ in range(axis_size("section")))), axis=0),
+            concat_axis=0,
+            split_axis=0,
+            axis_name="section",
+        ),
+        axis=0,
+    )
 
 
 def exchange(x, axes):
@@ -62,7 +75,7 @@
     gains_own = lax.dynamic_index_in_dim(gains_own, dp_index, 1, keepdims=False).reshape(
         1, rows_local
     )
-    gains = lax.all_gather(gains_own, "section", axis=0, tiled=True)
+    gains = _prepare_vectors(gains_own)
     fresh = lax.dynamic_slice_in_dim(activations, section_index * tok_part, tok_part, 0)
     fresh = exchange(fresh.reshape(tok_part, dps, own).transpose(1, 0, 2), "dp")
     current = fresh.reshape(tok_group, own).T

time: 360 us -> 360 us (level)
  blocking collectives: 196 us -> 185 us
  waiting for transfers between devices: 38.3 us -> 43.5 us
  starting transfers between devices: 35.6 us -> 40.4 us
    all_gather x1 -> x0, blocking collectives: 10.7 us -> none  [per_device(): gains = lax.all_gather(gains_own, 'section', axis=0, tiled=True)]
    all_to_all x0 -> x1, starting transfers between devices: none -> 4.8 us  [_prepare_vectors(): all_to_all(jnp.stack(tuple((packet for _ in range(axis_size('section'))))...]
    all_to_all x8, waiting for transfers between devices: 35.1 us -> 39 us  [exchange(): return lax.all_to_all(x, axes, 0, 0, tiled=True)]
  transfers between devices with their start and end apart: 9 -> 10, of which waited for: 6 -> 7; matrix products, arithmetic and copies ran while one was open for 6% -> 6% of each run, Pallas kernels for 0% -> 0%
where the time goes in v1:
time: 360 us; the launch traced here: 359 us
  blocking collectives  185 us (51%)
  waiting for transfers between devices  43.5 us (12%)
  starting transfers between devices  40.4 us (11%)
  local copies, waits for them, and re-layouts  32.6 us (9%)
  other arithmetic  28.4 us (8%)
  between operations  18.2 us (5%)
  matrix products  11 us (3%)
    all_gather x4, blocking collectives, per_device(): lax.all_gather(current, TENSOR, axis=0, tiled=True).astype(jnp.float32)  130 us
    all_to_all x8, waiting for transfers between devices, exchange(): return lax.all_to_all(x, axes, 0, 0, tiled=True)  39 us
    all_gather x1, blocking collectives, per_device(): target_all = lax.all_gather(targets[0], 'dp', axis=0)  35.7 us
    all_to_all x8, starting transfers between devices, exchange(): return lax.all_to_all(x, axes, 0, 0, tiled=True)  35.5 us
    all_to_all x1, blocking collectives, exchange(): return lax.all_to_all(x, axes, 0, 0, tiled=True)  19.5 us
    dot_general x5, local copies, waits for them, and re-layouts, per_device(): lax.dot_general(weights[block], scaled, (((0,), (0,)), ((), ())), preferr...  13.4 us
  transfers between devices with their start and end apart: 10, of which 7 were waited for; matrix products, arithmetic and copies ran while one was open for 6% of the time, Pallas kernels for 0%

profile of v1, /device:TPU:4, one launch (start us, length us, event | category | flops | bytes accessed | tf_op | source)
XLA Modules:
  0.0 358.8 jit_solution(8259019507140550224)
XLA Ops:
  7.2 2.7 shift_right_arithmetic.24
  10.0 3.1 shift_right_arithmetic.25
  13.1 1.9 add_clamp_fusion
  15.1 2.8 fusion.27
  18.0 19.5 %all_to_all.50 = bf16[4,512,256]{2,1,0:T(8,128)(2,1)} all-to-all(bf16[4,512,256]{2,1,0:T(8,128)(2,1)S(1)} %bitcast.121), channel_id=1, replica_groups=mesh['section'=4,'dp'=4,'tensor_0'=16,'tensor_1'=2] {'dp'}, dimensions={0} | all-to-all | bytes 2097152 | tf_op jit(solution)/shard_map/all_to_all | solution.py:30
  37.6 0.7 reshape.174
  38.3 3.3 all-to-all-start
  41.6 0.5 broadcast.144
  42.1 0.7 reduce.8
  43.0 3.8 %all-to-all-done = bf16[4,2,1024]{2,1,0:T(2,128)(2,1)S(1)} async-done(((bf16[4,2,1024]{2,1,0:T(2,128)(2,1)}), bf16[4,2,1024]{2,1,0:T(2,128)(2,1)S(1)}, u32[]{:S(2)}, u32[]{:S(2)}) %all-to-all-start) | async-done | bytes 16416 | tf_op jit(solution)/shard_map/all_to_all | solution.py:30
  46.9 0.6 stack.15
  47.5 4.8 %all-to-all-start.2 = ((f32[4,1,2048]{2,1,0:T(1,128)}), f32[4,1,2048]{2,1,0:T(1,128)S(1)}, u32[]{:S(2)}, u32[]{:S(2)}) async-start(f32[4,1,2048]{2,1,0:T(1,128)} %stack.15), calls=%async_computation.2 | async-start | bytes 65536 | tf_op jit(solution)/shard_map/all_to_all | solution.py:19
  52.5 37.7 %all_gather.18 = bf16[2048,128]{1,0:T(8,128)(2,1)S(1)} all-gather(bf16[64,128]{1,0:T(8,128)(2,1)S(1)} %bitcast.134), channel_id=1, replica_groups=mesh['section'=4,'dp'=4,'tensor_0'=16,'tensor_1'=2] {'tensor_0','tensor_1'}, dimensions={0}, use_global_device_ids=true | all-gather | bytes 540672 | tf_op jit(solution)/shard_map/all_gather | solution.py:87
  90.5 4.5 %all-gather.2.cloned.1.call-done = bf16[4,2048,256]{2,1,0:T(8,128)(2,1)} async-done(((bf16[1,2048,256]{2,1,0:T(8,128)(2,1)}), bf16[4,2048,256]{2,1,0:T(8,128)(2,1)}) %all-gather.2.cloned.1.call-update) | async-done | bytes 4194320 | tf_op jit(solution)/shard_map/all_gather | solution.py:73
  95.0 4.3 %slice_bitcast_fusion = (bf16[256,2048]{0,1:T(8,128)(2,1)}, bf16[256,2048]{0,1:T(8,128)(2,1)}, bf16[256,2048]{0,1:T(8,128)(2,1)}, bf16[256,2048]{0,1:T(8,128)(2,1)}) fusion(bf16[4,2048,256]{2,1,0:T(8,128)(2,1)} %all-gather.2.cloned.1.call-done), kind=kLoop, calls=%fused_computation.50 | loop fusion | bytes 8388608 | tf_op jit(solution)/shard_map/dot_general | solution.py:90
  99.3 2.3 copy.53
  101.6 1.8 fusion.38
  103.4 0.7 pad_maximum_fusion
  104.0 4.3 %all-to-all-start.3 = ((f32[4,72,128]{2,1,0:T(8,128)}), f32[4,72,128]{2,1,0:T(8,128)S(1)}, u32[]{:S(2)}, u32[]{:S(2)}) async-start(f32[4,72,128]{2,1,0:T(8,128)} %pad_maximum_fusion), calls=%async_computation.3 | async-start | bytes 294912 | tf_op jit(solution)/shard_map/all_to_all | solution.py:30
  108.3 2.3 copy.54
  110.6 2.3 copy.55
  112.9 2.3 copy.56
  115.2 32.4 %all_gather.20 = bf16[2048,128]{1,0:T(8,128)(2,1)S(1)} all-gather(bf16[64,128]{1,0:T(8,128)(2,1)S(1)} %fusion.53), channel_id=1, replica_groups=mesh['section'=4,'dp'=4,'tensor_0'=16,'tensor_1'=2] {'tensor_0','tensor_1'}, dimensions={0}, use_global_device_ids=true | all-gather | bytes 540672 | tf_op jit(solution)/shard_map/all_gather | solution.py:87
  147.9 1.8 fusion.35
  149.7 0.7 pad_maximum_fusion.1
  150.4 4.8 %all-to-all-start.4 = ((f32[4,72,128]{2,1,0:T(8,128)}), f32[4,72,128]{2,1,0:T(8,128)S(1)}, u32[]{:S(2)}, u32[]{:S(2)}) async-start(f32[4,72,128]{2,1,0:T(8,128)} %pad_maximum_fusion.1), calls=%async_computation.4 | async-start | bytes 294912 | tf_op jit(solution)/shard_map/all_to_all | solution.py:30
  155.2 1.1 fusion.14
  156.3 4.9 %all-to-all-done.4 = f32[4,72,128]{2,1,0:T(8,128)S(1)} async-done(((f32[4,72,128]{2,1,0:T(8,128)}), f32[4,72,128]{2,1,0:T(8,128)S(1)}, u32[]{:S(2)}, u32[]{:S(2)}) %all-to-all-start.4) | async-done | bytes 147488 | tf_op jit(solution)/shard_map/all_to_all | solution.py:30
  161.3 29.5 %all_gather.21 = bf16[2048,128]{1,0:T(8,128)(2,1)S(1)} all-gather(bf16[64,128]{1,0:T(8,128)(2,1)S(1)} %fusion.51), channel_id=1, replica_groups=mesh['section'=4,'dp'=4,'tensor_0'=16,'tensor_1'=2] {'tensor_0','tensor_1'}, dimensions={0}, use_global_device_ids=true | all-gather | bytes 540672 | tf_op jit(solution)/shard_map/all_gather | solution.py:87
  191.1 1.8 fusion.32
  192.9 0.7 pad_maximum_fusion.2
  193.6 3.3 all-to-all-start.5
  196.9 1.1 fusion.18
  198.1 5.0 %all-to-all-done.5 = f32[4,72,128]{2,1,0:T(8,128)S(1)} async-done(((f32[4,72,128]{2,1,0:T(8,128)}), f32[4,72,128]{2,1,0:T(8,128)S(1)}, u32[]{:S(2)}, u32[]{:S(2)}) %all-to-all-start.5) | async-done | bytes 147488 | tf_op jit(solution)/shard_map/all_to_all | solution.py:30
  203.2 30.0 %all_gather.22 = bf16[2048,128]{1,0:T(8,128)(2,1)S(1)} all-gather(bf16[64,128]{1,0:T(8,128)(2,1)S(1)} %fusion.49), channel_id=1, replica_groups=mesh['section'=4,'dp'=4,'tensor_0'=16,'tensor_1'=2] {'tensor_0','tensor_1'}, dimensions={0}, use_global_device_ids=true | all-gather | bytes 540672 | tf_op jit(solution)/shard_map/all_gather | solution.py:87
  233.5 1.8 fusion.29
  235.3 0.7 pad_maximum_fusion.3
  236.0 3.5 all-to-all-start.6
  239.5 1.1 fusion.22
  240.6 4.9 %all-to-all-done.6 = f32[4,72,128]{2,1,0:T(8,128)S(1)} async-done(((f32[4,72,128]{2,1,0:T(8,128)}), f32[4,72,128]{2,1,0:T(8,128)S(1)}, u32[]{:S(2)}, u32[]{:S(2)}) %all-to-all-start.6) | async-done | bytes 147488 | tf_op jit(solution)/shard_map/all_to_all | solution.py:30
  245.5 0.3 fusion.26
  245.9 6.8 %maximum_maximum_fusion = bf16[16,576,128]{2,1,0:T(8,128)(2,1)} fusion(bf16[4,64,128]{2,1,0:T(8,128)(2,1)S(1)} %broadcast_in_dim.29, bf16[4,512,128]{2,1,0:T(8,128)(2,1)S(1)} %bitcast.125, bf16[4,64,128]{2,1,0:T(8,128)(2,1)S(1)} %broadcast_in_dim.27, bf16[4,512,128]{2,1,0:T(8,128)(2,1)} %bitcast.124, bf16[4,64,128]{2,1,0:T(8,128)(2,1)S(1)} %broadcast_in_dim.25, ...), kind=kLoop, calls=%fused_computation.5 | loop fusion | flops 18874368 | bytes 4718592 | tf_op jit(solution)/shard_map/concatenate | solution.py:114
  252.8 5.8 %all-to-all-start.7 = ((bf16[16,576,128]{2,1,0:T(8,128)(2,1)}), bf16[16,576,128]{2,1,0:T(8,128)(2,1)}, u32[]{:S(2)}, u32[]{:S(2)}) async-start(bf16[16,576,128]{2,1,0:T(8,128)(2,1)} %maximum_maximum_fusion), calls=%async_computation.7 | async-start | bytes 4718592 | tf_op jit(solution)/shard_map/all_to_all | solution.py:30
  258.6 35.7 %all_gather.23 = bf16[4,128,256]{2,1,0:T(8,128)(2,1)S(1)} all-gather(bf16[1,128,256]{2,1,0:T(8,128)(2,1)S(1)} %copy-done.3), channel_id=1, replica_groups=mesh['section'=4,'dp'=4,'tensor_0'=16,'tensor_1'=2] {'dp'}, dimensions={0}, use_global_device_ids=true | all-gather | bytes 327680 | tf_op jit(solution)/shard_map/all_gather | solution.py:82
  294.3 0.8 copy_bitcast_fusion
  295.1 1.5 reshape.149
  296.6 1.1 copy.59
  297.7 1.5 fusion.4
  299.2 1.7 slice.111
  301.0 2.0 copy.57
  303.0 1.7 multiply_reduce_fusion.1
  304.9 3.9 %multiply_reduce_fusion = (f32[]{:T(128)}, f32[2048,256]{1,0:T(8,128)}) fusion(bf16[32,8,4,128]{3,2,1,0:T(4,128)(2,1)S(1)} %bitcast.133, bf16[256,8,4,128]{3,2,1,0:T(4,128)(2,1)S(1)} %bitcast.126, f32[256]{0:T(256)S(1)} %bitcast.147, f32[1,2048,256]{2,1,0:T(8,128)S(1)} %copy-done.1), kind=kOutput, calls=%fused_computation.18 | convolution fusion | flops 548405248 | bytes 6554628 | tf_op jit(solution)/shard_map/dot_general | solution.py:121
  309.4 1.3 select_maximum_fusion
  310.7 0.7 broadcast_in_dim_broadcast_in_dim_broadcast_in_dim.2
  311.4 7.3 %all-to-all-start.8 = ((f32[32,8,128]{2,1,0:T(8,128)}), f32[32,8,128]{2,1,0:T(8,128)S(1)}, u32[]{:S(2)}, u32[]{:S(2)}) async-start(f32[32,8,128]{2,1,0:T(8,128)} %broadcast_in_dim_broadcast_in_dim_broadcast_in_dim.2), calls=%async_computation.8 | async-start | bytes 262144 | tf_op jit(solution)/shard_map/all_to_all | solution.py:30
  318.7 1.0 slice_bitcast_fusion.4
  320.0 0.3 reshape_reshape.3
  320.3 15.6 %all-to-all-done.8 = f32[32,8,128]{2,1,0:T(8,128)S(1)} async-done(((f32[32,8,128]{2,1,0:T(8,128)}), f32[32,8,128]{2,1,0:T(8,128)S(1)}, u32[]{:S(2)}, u32[]{:S(2)}) %all-to-all-start.8) | async-done | bytes 131104 | tf_op jit(solution)/shard_map/all_to_all | solution.py:30
  336.0 0.6 broadcast_in_dim.30
  336.6 3.2 all-to-all-start.9
  339.8 0.6 constant_dynamic-slice_fusion
  340.5 4.7 %all-to-all-done.9 = f32[4,8,128]{2,1,0:T(8,128)S(1)} async-done(((f32[4,8,128]{2,1,0:T(8,128)}), f32[4,8,128]{2,1,0:T(8,128)S(1)}, u32[]{:S(2)}, u32[]{:S(2)}) %all-to-all-start.9) | async-done | bytes 16416 | tf_op jit(solution)/shard_map/all_to_all | solution.py:30
  345.1 0.6 fusion.67
  347.7 3.2 fusion.10
  (58 shorter events, 2.6 us)
Async XLA Ops:
  7.2 30.3 %copy-start = (bf16[128,256]{1,0:T(8,128)(2,1)S(1)}, bf16[128,256]{1,0:T(8,128)(2,1)}, u32[]{:S(2)}) copy-start(bf16[128,256]{1,0:T(8,128)(2,1)} %param.6) | copy-start | bytes 196612
  7.2 87.8 %all-gather.2.cloned.1.call-start = ((), (), s32[]{:S(2)}) async-start(), calls=%async_computation.10 | async-start | bytes 5242880 | tf_op jit(solution)/shard_map/all_gather | solution.py:73
  10.0 3.1 copy-start.1
  13.1 2.0 copy-start.5
  18.0 24.1 %copy-start.4 = (f32[1,8192]{1,0:T(1,128)S(1)}, f32[1,8192]{1,0:T(1,128)}, u32[]{:S(2)}) copy-start(f32[1,8192]{1,0:T(1,128)} %param.11) | copy-start | bytes 98308
  38.3 8.6 %all-to-all-start = ((bf16[4,2,1024]{2,1,0:T(2,128)(2,1)}), bf16[4,2,1024]{2,1,0:T(2,128)(2,1)S(1)}, u32[]{:S(2)}, u32[]{:S(2)}) async-start(bf16[4,2,1024]{2,1,0:T(2,128)(2,1)} %reshape.174), calls=%async_computation | async-start | bytes 32768 | tf_op jit(solution)/shard_map/all_to_all | solution.py:30
  47.5 42.9 %all-to-all-start.2 = ((f32[4,1,2048]{2,1,0:T(1,128)}), f32[4,1,2048]{2,1,0:T(1,128)S(1)}, u32[]{:S(2)}, u32[]{:S(2)}) async-start(f32[4,1,2048]{2,1,0:T(1,128)} %stack.15), calls=%async_computation.2 | async-start | bytes 65536 | tf_op jit(solution)/shard_map/all_to_all | solution.py:19
  104.0 11.1 %all-to-all-start.3 = ((f32[4,72,128]{2,1,0:T(8,128)}), f32[4,72,128]{2,1,0:T(8,128)S(1)}, u32[]{:S(2)}, u32[]{:S(2)}) async-start(f32[4,72,128]{2,1,0:T(8,128)} %pad_maximum_fusion), calls=%async_computation.3 | async-start | bytes 294912 | tf_op jit(solution)/shard_map/all_to_all | solution.py:30
  150.4 10.9 %all-to-all-start.4 = ((f32[4,72,128]{2,1,0:T(8,128)}), f32[4,72,128]{2,1,0:T(8,128)S(1)}, u32[]{:S(2)}, u32[]{:S(2)}) async-start(f32[4,72,128]{2,1,0:T(8,128)} %pad_maximum_fusion.1), calls=%async_computation.4 | async-start | bytes 294912 | tf_op jit(solution)/shard_map/all_to_all | solution.py:30
  193.6 9.5 %all-to-all-start.5 = ((f32[4,72,128]{2,1,0:T(8,128)}), f32[4,72,128]{2,1,0:T(8,128)S(1)}, u32[]{:S(2)}, u32[]{:S(2)}) async-start(f32[4,72,128]{2,1,0:T(8,128)} %pad_maximum_fusion.2), calls=%async_computation.5 | async-start | bytes 294912 | tf_op jit(solution)/shard_map/all_to_all | solution.py:30
  236.0 9.5 %all-to-all-start.6 = ((f32[4,72,128]{2,1,0:T(8,128)}), f32[4,72,128]{2,1,0:T(8,128)S(1)}, u32[]{:S(2)}, u32[]{:S(2)}) async-start(f32[4,72,128]{2,1,0:T(8,128)} %pad_maximum_fusion.3), calls=%async_computation.6 | async-start | bytes 294912 | tf_op jit(solution)/shard_map/all_to_all | solution.py:30
  252.8 5.8 %copy-start.3 = (bf16[1,128,256]{2,1,0:T(8,128)(2,1)S(1)}, bf16[1,128,256]{2,1,0:T(8,128)(2,1)}, u32[]{:S(2)}) copy-start(bf16[1,128,256]{2,1,0:T(8,128)(2,1)} %param.7) | copy-start | bytes 196612
  252.8 46.4 %all-to-all-start.7 = ((bf16[16,576,128]{2,1,0:T(8,128)(2,1)}), bf16[16,576,128]{2,1,0:T(8,128)(2,1)}, u32[]{:S(2)}, u32[]{:S(2)}) async-start(bf16[16,576,128]{2,1,0:T(8,128)(2,1)} %maximum_maximum_fusion), calls=%async_computation.7 | async-start | bytes 4718592 | tf_op jit(solution)/shard_map/all_to_all | solution.py:30
  301.0 2.0 copy-start.2
  311.4 24.5 %all-to-all-start.8 = ((f32[32,8,128]{2,1,0:T(8,128)}), f32[32,8,128]{2,1,0:T(8,128)S(1)}, u32[]{:S(2)}, u32[]{:S(2)}) async-start(f32[32,8,128]{2,1,0:T(8,128)} %broadcast_in_dim_broadcast_in_dim_broadcast_in_dim.2), calls=%async_computation.8 | async-start | bytes 262144 | tf_op jit(solution)/shard_map/all_to_all | solution.py:30
  336.6 8.6 %all-to-all-start.9 = ((f32[4,8,128]{2,1,0:T(8,128)}), f32[4,8,128]{2,1,0:T(8,128)S(1)}, u32[]{:S(2)}, u32[]{:S(2)}) async-start(f32[4,8,128]{2,1,0:T(8,128)} %broadcast_in_dim.30), calls=%async_computation.9 | async-start | bytes 32768 | tf_op jit(solution)/shard_map/all_to_all | solution.py:30
Sparse Core Ops, SparseCore 0:
  37.6 57.3 all-gather.1
